TPU v7x, 512 devices: a whole 4x8x8 slice. The times are simulated.
512 devices in a mesh: vocab: 64 (over y, x, core), width: 8 (over z).
Axes of the slice: x: 4, y: 8, z: 8, core: 2. Of those that a mesh axis runs over, the one named last changes fastest.
Arguments:
- hidden: bfloat16 [8192, 2048], P('vocab', 'width'), may hold values from -400 to 400
- norm_gain: bfloat16 [2048], P('width'), may hold values from 0.5 to 1.5
- head_weight: bfloat16 [102400, 2048], P('vocab', 'width'), may hold values from -1 to 1
- targets: int32 [8192], P(('vocab', 'width')), may hold values from 0 to 102399
- pad_mask: int32 [8192], P(('vocab', 'width')), may hold values 0 or 1
- lengths: int32 [64], replicated, may hold values from 1 to 2048, 8192 in all
Outputs:
- entropy: float32 [8192], P(('vocab', 'width'))
- token_logprob: float32 [8192], P(('vocab', 'width'))
- seq_score: float32 [64], replicated
Inputs may be any that keep to these rules, and one draw needn't show every extreme that they name: The lengths sum to 8192.
All inputs are finite; a program needn't handle non-finite values. No bound on the sum of `pad_mask` on one device may be relied on, other than what follows from the above.
Results may differ from a plain program's by a relative error of at most 0.0031.
Values may be sent and summed in bfloat16 or wider, within the bound.
A program may use at most 64 MiB of HBM per device.

v0:
```python
import math
import jax
import jax.numpy as jnp
from jax import lax
from jax.sharding import PartitionSpec as P

epsilon = 1e-06


def merged_2(value, axis, join):
    pieces = jax.tree.map(lambda part: lax.all_gather(part, axis), value)
    head = jax.tree.map(lambda part: part[0], pieces)
    tail = jax.tree.map(lambda part: part[1:], pieces)
    total, _ = lax.scan(lambda total, piece: (join(total, piece), None), head, tail)
    return total


def summarize(logits, block_ids, first_col):
    peak = jnp.max(logits, axis=1)
    shifted = logits - peak[:, None]
    weights = jnp.exp(shifted)
    exp_total = jnp.sum(weights, axis=1)
    spread = jnp.sum(weights * shifted, axis=1)
    columns = first_col + lax.iota(jnp.int32, logits.shape[1])
    target_logit = jnp.sum(jnp.where(columns[None, :] == block_ids[:, None], logits, 0.0), axis=1)
    return (peak, exp_total, spread, target_logit)


def combine(earlier, later):
    peak = jnp.maximum(earlier[0], later[0])
    left_lift = jnp.exp(earlier[0] - peak)
    right_lift = jnp.exp(later[0] - peak)
    exp_total = earlier[1] * left_lift + later[1] * right_lift
    spread = left_lift * (earlier[2] + (earlier[0] - peak) * earlier[1]) + right_lift * (
        later[2] + (later[0] - peak) * later[1]
    )
    return (peak, exp_total, spread, earlier[3] + later[3])


def per_device(hidden, norm_gain, head_weight, targets, pad_mask, lengths):
    width_count = lax.axis_size("width")
    own_count = targets.shape[0]
    values = hidden.astype(jnp.float32)
    energy = lax.psum(jnp.sum(values * values, axis=1), "width")
    inv_rms = lax.rsqrt(energy / (hidden.shape[1] * width_count) + epsilon)
    normed = (values * inv_rms[:, None] * norm_gain.astype(jnp.float32)[None, :]).astype(
        jnp.bfloat16
    )
    full_rows = lax.all_to_all(normed, "width", split_axis=0, concat_axis=1, tiled=True)
    gathered, gathered_ids = (
        lax.all_gather(full_rows, "vocab", axis=0, tiled=True),
        lax.all_gather(targets, "vocab", axis=0, tiled=True),
    )
    col_count = head_weight.shape[0]
    first_col = lax.axis_index("vocab") * col_count
    total_rows = gathered.shape[0]
    block_rows = math.gcd(total_rows, 512)
    contract = (((1,), (1,)), ((), ()))
    head_full = lax.all_gather(head_weight, "width", axis=1, tiled=True)

    def per_block(inputs):
        logits = lax.dot_general(inputs[0], head_full, contract, preferred_element_type=jnp.float32)
        return summarize(logits, inputs[1], first_col)

    blocked = lax.map(
        per_block,
        (gathered.reshape(-1, block_rows, gathered.shape[1]), gathered_ids.reshape(-1, block_rows)),
    )
    statistics = (
        blocked[0].reshape(-1),
        blocked[1].reshape(-1),
        blocked[2].reshape(-1),
        blocked[3].reshape(-1),
    )
    merged = merged_2(statistics, "vocab", combine)
    own_start = lax.axis_index("vocab") * own_count
    peak = lax.dynamic_slice_in_dim(merged[0], own_start, own_count, 0)
    exp_total = lax.dynamic_slice_in_dim(merged[1], own_start, own_count, 0)
    spread = lax.dynamic_slice_in_dim(merged[2], own_start, own_count, 0)
    target_logit = lax.dynamic_slice_in_dim(merged[3], own_start, own_count, 0)
    kept_mask = pad_mask.astype(jnp.float32)
    log_total = jnp.log(exp_total)
    entropy = kept_mask * (log_total - spread / exp_total)
    token_logprob = kept_mask * (target_logit - peak - log_total)
    device_index = lax.axis_index("vocab") * width_count + lax.axis_index("width")
    token_index = device_index * own_count + lax.iota(jnp.int32, own_count)
    seq_ends = jnp.cumsum(lengths)
    seq_starts = seq_ends - lengths
    member = (
        (token_index[:, None] >= seq_starts[None, :]) & (token_index[:, None] < seq_ends[None, :])
    ).astype(jnp.float32)
    partial_value = jnp.sum(member * token_logprob[:, None], axis=0)
    seq_score = lax.psum(partial_value, ("vocab", "width")) / lengths.astype(jnp.float32)
    return (entropy, token_logprob, seq_score)


def solution(mesh):
    placed = (
        P("vocab", "width"),
        P("width"),
        P("vocab", "width"),
        P(("vocab", "width")),
        P(("vocab", "width")),
        P(),
    )
    return jax.shard_map(
        per_device,
        mesh=mesh,
        in_specs=placed,
        out_specs=(P(("vocab", "width")), P(("vocab", "width")), P()),
        check_vma=False,
    )
```

profile of v0, /device:TPU:1, one launch (start us, length us, event | category | flops | bytes accessed | tf_op | source)
XLA Modules:
  0.0 491.1 jit_solution(4575408305845917003)
XLA Ops:
  7.2 0.0 all-gather.7.cloned.1.call-start
  7.2 0.9 fusion.5
  8.2 20.3 %psum.14 = f32[128]{0:T(128)S(1)} all-reduce(f32[128]{0:T(128)S(1)} %fusion.5), channel_id=1, replica_groups=mesh['vocab'=64,'width'=8] {'width'}, use_global_device_ids=true, to_apply=%region_1.0 | all-reduce | flops 128 | bytes 1024 | tf_op jit(solution)/shard_map/psum | solution.py:44
  28.4 0.7 convert_element_type.18
  29.1 0.9 fusion.7
  30.0 9.6 %all_to_all.19 = bf16[8,16,256]{2,1,0:T(8,128)(2,1)S(1)} all-to-all(bf16[8,16,256]{2,1,0:T(8,128)(2,1)S(1)} %bitcast.73), channel_id=1, replica_groups=mesh['vocab'=64,'width'=8] {'width'}, dimensions={0} | all-to-all | bytes 131072 | tf_op jit(solution)/shard_map/all_to_all | solution.py:49
  39.6 0.6 copy.21
  40.2 0.0 all-gather.7.cloned.1.call-update
  40.3 0.0 all-gather.9.cloned.1.call-start
  40.3 0.7 all-gather.9.cloned.1.call-update
  41.1 1.3 dynamic-slice
  43.0 0.9 dynamic-update-slice
  43.9 22.5 %all-reduce = s32[1024]{0:T(1024)S(1)} all-reduce(s32[1024]{0:T(1024)S(1)} %dynamic-update-slice), channel_id=1, replica_groups=mesh['vocab'=64,'width'=8] {'vocab'}, use_global_device_ids=true, to_apply=%add | all-reduce | flops 1024 | bytes 8192
  66.4 0.7 copy.16
  67.2 0.1 reduce-window.8
  67.3 0.1 reduce
  67.4 0.7 sub.31
  68.0 58.4 %all-gather.7.cloned.1.call-done = bf16[1024,2048]{1,0:T(8,128)(2,1)} async-done(((bf16[16,2048]{1,0:T(8,128)(2,1)}), bf16[1024,2048]{1,0:T(8,128)(2,1)}) %all-gather.7.cloned.1.call-update) | async-done | bytes 4194320 | tf_op jit(solution)/shard_map/all_gather | solution.py:51
  126.4 83.2 %all-gather.9.cloned.1.call-done = bf16[1600,2048]{1,0:T(8,128)(2,1)} async-done(((bf16[1600,256]{1,0:T(8,128)(2,1)}), bf16[1600,2048]{1,0:T(8,128)(2,1)}) %all-gather.9.cloned.1.call-update) | async-done | bytes 6553616 | tf_op jit(solution)/shard_map/all_gather | solution.py:59
  209.6 16.2 %while.32 = (s32[]{:T(128)}, f32[2,512]{1,0:T(2,128)S(1)}, f32[2,512]{1,0:T(2,128)S(1)}, f32[2,512]{1,0:T(2,128)S(1)}, f32[2,512]{1,0:T(2,128)S(1)}, /*index=5*/...) while((s32[]{:T(128)}, f32[2,512]{1,0:T(2,128)S(1)}, ...), condition=%wide.region_7.8_spmd, body=%wide.region_2.7_spmd.sunk | while | flops 3361996288 | bytes 15250565 | solution.py:65
  209.6 6.4 %fusion.14 = (f32[512]{0:T(512)S(1)}, f32[512,1600]{0,1:T(8,128)S(1)}) fusion(bf16[1600,2048]{1,0:T(8,128)(2,1)} %get-tuple-element.320, bf16[2,512,2048]{2,1,0:T(8,128)(2,1)} %get-tuple-element.319, s32[]{:T(128)} %get-tuple-element.303), kind=kOutput, calls=%fused_computation.31.clone.1 | convolution fusion | flops 3356261888 | bytes 11930112 | tf_op jit(solution)/shard_map/while/body/eval_jaxpr/dot_general | solution.py:62
  216.1 1.4 fusion.15
  217.7 6.4 %fusion.14 = (f32[512]{0:T(512)S(1)}, f32[512,1600]{0,1:T(8,128)S(1)}) fusion(bf16[1600,2048]{1,0:T(8,128)(2,1)} %get-tuple-element.320, bf16[2,512,2048]{2,1,0:T(8,128)(2,1)} %get-tuple-element.319, s32[]{:T(128)} %get-tuple-element.303), kind=kOutput, calls=%fused_computation.31.clone.1 | convolution fusion | flops 3356261888 | bytes 11930112 | tf_op jit(solution)/shard_map/while/body/eval_jaxpr/dot_general | solution.py:62
  224.2 1.4 fusion.15
  225.8 0.0 copy-start.2
  225.8 0.0 copy-start.1
  225.8 42.7 %all-gather = f32[64,1,1024]{2,1,0:T(1,128)S(1)} all-gather(f32[1,1,1024]{2,1,0:T(1,128)S(1)} %reshape.60), channel_id=1, replica_groups=mesh['vocab'=64,'width'=8] {'vocab'}, dimensions={0}, use_global_device_ids=true | all-gather | bytes 266240 | tf_op jit(solution)/shard_map/all_gather | solution.py:11
  268.6 37.2 %all-gather.1 = f32[64,1,1024]{2,1,0:T(1,128)S(1)} all-gather(f32[1,1,1024]{2,1,0:T(1,128)S(1)} %reshape.62), channel_id=1, replica_groups=mesh['vocab'=64,'width'=8] {'vocab'}, dimensions={0}, use_global_device_ids=true | all-gather | bytes 266240 | tf_op jit(solution)/shard_map/all_gather | solution.py:11
  305.8 36.9 %all-gather.2 = f32[64,1,1024]{2,1,0:T(1,128)S(1)} all-gather(f32[1,1,1024]{2,1,0:T(1,128)S(1)} %reshape.64), channel_id=1, replica_groups=mesh['vocab'=64,'width'=8] {'vocab'}, dimensions={0}, use_global_device_ids=true | all-gather | bytes 266240 | tf_op jit(solution)/shard_map/all_gather | solution.py:11
  342.7 37.1 %all-gather.3 = f32[64,1,1024]{2,1,0:T(1,128)S(1)} all-gather(f32[1,1,1024]{2,1,0:T(1,128)S(1)} %reshape.66), channel_id=1, replica_groups=mesh['vocab'=64,'width'=8] {'vocab'}, dimensions={0}, use_global_device_ids=true | all-gather | bytes 266240 | tf_op jit(solution)/shard_map/all_gather | solution.py:11
  380.2 7.6 %while.33 = (s32[]{:T(128)}, f32[1024]{0:T(1024)S(1)}, f32[1024]{0:T(1024)S(1)}, f32[1024]{0:T(1024)S(1)}, f32[1024]{0:T(1024)S(1)}, /*index=5*/f32[63,1024]{1,0...) while((s32[]{:T(128)}, f32[1024]{0:T(1024)S(1)}, ...), condition=%wide.region_9.10_spmd, body=%wide.region_8.9_spmd.sunk | while | flops 16386 | bytes 110701 | solution.py:14
  387.7 0.0 copy-done.2
  387.7 0.6 subtract_multiply_fusion
  388.3 0.0 copy-start
  388.3 0.1 select_reduce_fusion.1
  388.4 95.3 %psum.15 = f32[64]{0:T(128)S(1)} all-reduce(f32[64]{0:T(128)S(1)} %select_reduce_fusion.1), channel_id=1, replica_groups=mesh['vocab'=64,'width'=8] {'vocab','width'}, use_global_device_ids=true, to_apply=%region_12.13 | all-reduce | flops 64 | bytes 512 | tf_op jit(solution)/shard_map/psum | solution.py:93
  483.7 0.0 copy-done.1
  483.7 0.5 convert_divide_fusion
  484.2 0.0 copy-done
  (414 shorter events, 4.6 us)
Async XLA Ops:
  7.2 119.3 %all-gather.7.cloned.1.call-start = ((), (), s32[]{:S(2)}) async-start(), calls=%async_computation.1 | async-start | bytes 4259840 | tf_op jit(solution)/shard_map/all_gather | solution.py:51
  40.3 169.3 %all-gather.9.cloned.1.call-start = ((), (), s32[]{:S(2)}) async-start(), calls=%async_computation.2 | async-start | bytes 7372800 | tf_op jit(solution)/shard_map/all_gather | solution.py:59
  225.8 162.0 %copy-start.2 = (s32[16]{0:T(128)S(1)}, s32[16]{0:T(128)}, u32[]{:S(2)}) copy-start(s32[16]{0:T(128)} %param.14) | copy-start | bytes 196
  225.8 257.9 %copy-start.1 = (s32[64]{0:T(128)S(1)}, s32[64]{0:T(128)}, u32[]{:S(2)}) copy-start(s32[64]{0:T(128)} %param.15) | copy-start | bytes 772
  388.3 95.9 %copy-start = (f32[16]{0:T(128)}, f32[16]{0:T(128)S(1)}, u32[]{:S(2)}) copy-start(f32[16]{0:T(128)S(1)} %get-tuple-element.158) | copy-start | bytes 196
Sparse Core Ops, SparseCore 0:
  40.4 85.9 all-gather.6
  128.4 81.1 all-gather.8
where the time goes:
time: 491 us
  blocking collectives  302 us (62%)
  waiting for transfers between devices  142 us (29%)
  between operations  14.9 us (3%)
  matrix products  12.9 us (3%)
  other arithmetic  9.19 us (2%)
  local copies, waits for them, and re-layouts  6.36 us (1%)
    all_gather x4, blocking collectives, merged_2(): pieces = jax.tree.map(lambda part: lax.all_gather(part, axis), value)  154 us
    psum x1, blocking collectives, per_device(): lax.psum(partial_value, ('vocab', 'width')) / lengths.astype(jnp.float32)  95.3 us
    all_gather x1, waiting for transfers between devices, per_device(): head_full = lax.all_gather(head_weight, 'width', axis=1, tiled=True)  83.2 us
    all_gather x1, waiting for transfers between devices, per_device(): lax.all_gather(full_rows, 'vocab', axis=0, tiled=True)  58.4 us
    unnamed x1, blocking collectives  22.5 us
    psum x1, blocking collectives, per_device(): energy = lax.psum(jnp.sum(values * values, axis=1), 'width')  20.3 us
    dot_general x2, matrix products, per_block(): lax.dot_general(inputs[0], head_full, contract, preferred_element_type=jn...  12.9 us
  transfers between devices with their start and end apart: 2, of which 2 were waited for; matrix products, arithmetic and copies ran while one was open for 1% of the time, Pallas kernels for 0%

commit v1 on v0

--- a/solution.py
+++ b/solution.py
@@ -5,6 +5,28 @@
 from jax.sharding import PartitionSpec as P
 
 epsilon = 1e-06
+
+
+def joined_along(blocks, dim):
+    shape = list(blocks.shape[1:])
+    shape[dim] *= blocks.shape[0]
+    return jnp.moveaxis(blocks, 0, dim).reshape(shape)
+
+
+def gather_around(value, axis, dim):
+    size = lax.axis_size(axis)
+    pairs = [(i, (i + 1) % size) for i in range(size)]
+    back = [(b, a) for a, b in pairs]
+    lower, upper = ([], [])
+    for step in range(size - 1):
+        if step % 2 == 0:
+            lower.append(lax.ppermute(lower[-1] if lower else value, axis, pairs))
+        else:
+            upper.append(lax.ppermute(upper[-1] if upper else value, axis, back))
+    blocks = jnp.stack([*lower[::-1], value, *upper])
+    shift = lax.axis_index(axis) - len(lower)
+    blocks = blocks[(jnp.arange(size) - shift) % size]
+    return joined_along(blocks, dim)
 
 
 def merged_2(value, axis, join):
@@ -56,7 +78,7 @@
     total_rows = gathered.shape[0]
     block_rows = math.gcd(total_rows, 512)
     contract = (((1,), (1,)), ((), ()))
-    head_full = lax.all_gather(head_weight, "width", axis=1, tiled=True)
+    head_full = gather_around(head_weight, "width", 1)
 
     def per_block(inputs):
         logits = lax.dot_general(inputs[0], head_full, contract, preferred_element_type=jnp.float32)

time: 491 us -> 442 us (0.900)
  waiting for transfers between devices: 142 us -> 39.7 us
  local copies, waits for them, and re-layouts: 6.36 us -> 30.4 us
  starting transfers between devices: 0.08 us -> 22.2 us
  blocking collectives: 302 us -> 307 us
    all_gather x1 -> x0, waiting for transfers between devices: 83.2 us -> none  [per_device(): head_full = lax.all_gather(head_weight, 'width', axis=1, tiled=True)]
    all_gather x1, waiting for transfers between devices: 58.4 us -> 0.01 us  [per_device(): lax.all_gather(full_rows, 'vocab', axis=0, tiled=True)]
    ppermute x0 -> x7, waiting for transfers between devices: none -> 39.7 us  [the longest x4 35.5 us: gather_around(): lower.append(lax.ppermute(lower[-1] if lower else value, axis, pairs))]
    ppermute x0 -> x7, starting transfers between devices: none -> 22.2 us  [the longest x3 14.3 us: gather_around(): upper.append(lax.ppermute(upper[-1] if upper else value, axis, back))]
    unnamed x17 -> x26, local copies, waits for them, and re-layouts: 2.41 us -> 12.5 us
    gather x0 -> x1, local copies, waits for them, and re-layouts: none -> 6.52 us  [gather_around(): blocks = blocks[(jnp.arange(size) - shift) % size]]
    reshape x0 -> x1, local copies, waits for them, and re-layouts: none -> 6.52 us  [joined_along(): return jnp.moveaxis(blocks, 0, dim).reshape(shape)]
    unnamed x1, blocking collectives: 22.5 us -> 27.8 us
  transfers between devices with their start and end apart: 2 -> 8, of which waited for: 2 -> 4; matrix products, arithmetic and copies ran while one was open for 1% -> 6% of each run, Pallas kernels for 0% -> 0%
where the time goes in v1:
time: 442 us; the launch traced here: 441 us
  blocking collectives  307 us (69%)
  waiting for transfers between devices  39.7 us (9%)
  local copies, waits for them, and re-layouts  30.4 us (7%)
  starting transfers between devices  22.2 us (5%)
  between operations  15 us (3%)
  matrix products  12.9 us (3%)
  other arithmetic  9.28 us (2%)
    all_gather x4, blocking collectives, merged_2(): pieces = jax.tree.map(lambda part: lax.all_gather(part, axis), value)  153 us
    psum x1, blocking collectives, per_device(): lax.psum(partial_value, ('vocab', 'width')) / lengths.astype(jnp.float32)  96.9 us
    ppermute x4, waiting for transfers between devices, gather_around(): lower.append(lax.ppermute(lower[-1] if lower else value, axis, pairs))  35.5 us
    unnamed x1, blocking collectives  27.8 us
    psum x1, blocking collectives, per_device(): energy = lax.psum(jnp.sum(values * values, axis=1), 'width')  20.3 us
    ppermute x3, starting transfers between devices, gather_around(): upper.append(lax.ppermute(upper[-1] if upper else value, axis, back))  14.3 us
    dot_general x2, matrix products, per_block(): lax.dot_general(inputs[0], head_full, contract, preferred_element_type=jn...  12.9 us
    unnamed x26, local copies, waits for them, and re-layouts  12.5 us
  transfers between devices with their start and end apart: 8, of which 4 were waited for; matrix products, arithmetic and copies ran while one was open for 6% of the time, Pallas kernels for 0%

profile of v1, /device:TPU:1, one launch (start us, length us, event | category | flops | bytes accessed | tf_op | source)
XLA Modules:
  0.0 440.7 jit_solution(9112587625399733994)
XLA Ops:
  7.2 1.0 fusion.5
  8.2 20.3 %psum.14 = f32[128]{0:T(128)S(1)} all-reduce(f32[128]{0:T(128)S(1)} %fusion.5), channel_id=1, replica_groups=mesh['vocab'=64,'width'=8] {'width'}, use_global_device_ids=true, to_apply=%region_1.0 | all-reduce | flops 128 | bytes 1024 | tf_op jit(solution)/shard_map/psum | solution.py:66
  28.5 0.7 convert_element_type.18
  29.2 0.9 fusion.7
  30.1 9.6 %all_to_all.19 = bf16[8,16,256]{2,1,0:T(8,128)(2,1)S(1)} all-to-all(bf16[8,16,256]{2,1,0:T(8,128)(2,1)S(1)} %bitcast.96), channel_id=1, replica_groups=mesh['vocab'=64,'width'=8] {'width'}, dimensions={0} | all-to-all | bytes 131072 | tf_op jit(solution)/shard_map/all_to_all | solution.py:71
  39.7 0.6 copy.25
  40.3 2.2 collective-permute-start
  42.6 15.0 %collective-permute-done = bf16[1600,256]{1,0:T(8,128)(2,1)S(1)} collective-permute-done((bf16[1600,256]{1,0:T(8,128)(2,1)}, bf16[1600,256]{1,0:T(8,128)(2,1)S(1)}, u32[]{:S(2)}, u32[]{:S(2)}) %collective-permute-start) | collective-permute-done | bytes 819232 | tf_op jit(solution)/shard_map/ppermute | solution.py:23
  57.6 1.9 collective-permute-start.1
  59.5 4.6 %collective-permute-start.4 = (bf16[1600,256]{1,0:T(8,128)(2,1)}, bf16[1600,256]{1,0:T(8,128)(2,1)S(1)}, u32[]{:S(2)}, u32[]{:S(2)}) collective-permute-start(bf16[1600,256]{1,0:T(8,128)(2,1)} %param.12), channel_id=1, source_target_pairs={{1,0},{2,1},{3,2},{4,3},{5,4},{6,5},{7,6},{0,7},{9,8},{10,9},{11,1... | collective-permute-start | bytes 2457608 | tf_op jit(solution)/shard_map/ppermute | solution.py:25
  64.1 10.2 %collective-permute-done.1 = bf16[1600,256]{1,0:T(8,128)(2,1)S(1)} collective-permute-done((bf16[1600,256]{1,0:T(8,128)(2,1)S(1)}, bf16[1600,256]{1,0:T(8,128)(2,1)S(1)}, u32[]{:S(2)}, u32[]{:S(2)}) %collective-permute-start.1) | collective-permute-done | bytes 819232 | tf_op jit(solution)/shard_map/ppermute | solution.py:23
  74.3 1.9 collective-permute-start.2
  76.2 4.6 %collective-permute-start.5 = (bf16[1600,256]{1,0:T(8,128)(2,1)S(1)}, bf16[1600,256]{1,0:T(8,128)(2,1)}, u32[]{:S(2)}, u32[]{:S(2)}) collective-permute-start(bf16[1600,256]{1,0:T(8,128)(2,1)S(1)} %collective-permute-done.4), channel_id=1, source_target_pairs={{1,0},{2,1},{3,2},{4,3},{5,4},{6,5},{7,6},{0,7},{9,8},{10,9},{11,1... | collective-permute-start | bytes 2457608 | tf_op jit(solution)/shard_map/ppermute | solution.py:25
  80.8 10.3 %collective-permute-done.2 = bf16[1600,256]{1,0:T(8,128)(2,1)} collective-permute-done((bf16[1600,256]{1,0:T(8,128)(2,1)S(1)}, bf16[1600,256]{1,0:T(8,128)(2,1)}, u32[]{:S(2)}, u32[]{:S(2)}) %collective-permute-start.2) | collective-permute-done | bytes 819232 | tf_op jit(solution)/shard_map/ppermute | solution.py:23
  91.1 1.9 collective-permute-start.3
  93.0 1.3 dynamic-slice
  95.0 0.9 dynamic-update-slice
  95.8 27.8 %all-reduce = s32[1024]{0:T(1024)S(1)} all-reduce(s32[1024]{0:T(1024)S(1)} %dynamic-update-slice), channel_id=1, replica_groups=mesh['vocab'=64,'width'=8] {'vocab'}, use_global_device_ids=true, to_apply=%add | all-reduce | flops 1024 | bytes 8192
  123.7 0.7 copy.20
  124.4 0.1 reduce-window.8
  124.5 0.1 reduce
  124.6 0.7 sub.50
  125.4 5.1 %collective-permute-start.6 = (bf16[1600,256]{1,0:T(8,128)(2,1)}, bf16[1600,256]{1,0:T(8,128)(2,1)S(1)}, u32[]{:S(2)}, u32[]{:S(2)}) collective-permute-start(bf16[1600,256]{1,0:T(8,128)(2,1)} %collective-permute-done.5), channel_id=1, source_target_pairs={{1,0},{2,1},{3,2},{4,3},{5,4},{6,5},{7,6},{0,7},{9,8},{10,9},{11,1... | collective-permute-start | bytes 2457608 | tf_op jit(solution)/shard_map/ppermute | solution.py:25
  130.5 2.1 bitcast_dynamic-update-slice_fusion.7
  132.6 2.1 bitcast_dynamic-update-slice_fusion.6
  134.7 1.0 bitcast_dynamic-update-slice_fusion.5
  135.7 0.9 bitcast_dynamic-update-slice_fusion.4
  136.6 0.9 bitcast_dynamic-update-slice_fusion.3
  137.6 0.9 bitcast_dynamic-update-slice_fusion.2
  138.5 2.1 bitcast_dynamic-update-slice_fusion.1
  140.6 4.1 collective-permute-done.6
  144.8 0.9 bitcast_dynamic-update-slice_fusion
  145.7 6.5 %gather_fusion = bf16[8,1600,256]{2,1,0:T(8,128)(2,1)} fusion(bf16[8,1600,256]{2,1,0:T(8,128)(2,1)} %bitcast_dynamic-update-slice_fusion, s32[1024]{0:T(1024)S(1)} %pad_clamp_fusion), kind=kCustom, calls=%fused_computation | custom fusion | bytes 13107232 | tf_op jit(solution)/shard_map/gather | solution.py:28
  152.2 6.5 %copy.26 = bf16[8,200,8,256]{3,2,0,1:T(8,128)(2,1)} copy(bf16[8,200,8,256]{3,2,1,0:T(8,128)(2,1)} %bitcast.81) | data formatting | bytes 13107200 | tf_op jit(solution)/shard_map/reshape | solution.py:13
  158.8 16.2 %while.32 = (s32[]{:T(128)}, f32[2,512]{1,0:T(2,128)S(1)}, f32[2,512]{1,0:T(2,128)S(1)}, f32[2,512]{1,0:T(2,128)S(1)}, f32[2,512]{1,0:T(2,128)S(1)}, /*index=5*/...) while((s32[]{:T(128)}, f32[2,512]{1,0:T(2,128)S(1)}, ...), condition=%wide.region_7.8_spmd, body=%wide.region_2.7_spmd.sunk | while | flops 3361996288 | bytes 15250565 | solution.py:87
  158.8 6.5 %fusion.16 = (f32[512]{0:T(512)S(1)}, f32[512,1600]{0,1:T(8,128)S(1)}) fusion(bf16[1600,2048]{1,0:T(8,128)(2,1)} %get-tuple-element.320, bf16[2,512,2048]{2,1,0:T(8,128)(2,1)} %get-tuple-element.319, s32[]{:T(128)} %get-tuple-element.303), kind=kOutput, calls=%fused_computation.47.clone.1 | convolution fusion | flops 3356261888 | bytes 11930112 | tf_op jit(solution)/shard_map/while/body/eval_jaxpr/dot_general | solution.py:84
  165.3 1.4 fusion.17
  166.9 6.4 %fusion.16 = (f32[512]{0:T(512)S(1)}, f32[512,1600]{0,1:T(8,128)S(1)}) fusion(bf16[1600,2048]{1,0:T(8,128)(2,1)} %get-tuple-element.320, bf16[2,512,2048]{2,1,0:T(8,128)(2,1)} %get-tuple-element.319, s32[]{:T(128)} %get-tuple-element.303), kind=kOutput, calls=%fused_computation.47.clone.1 | convolution fusion | flops 3356261888 | bytes 11930112 | tf_op jit(solution)/shard_map/while/body/eval_jaxpr/dot_general | solution.py:84
  173.3 1.4 fusion.17
  174.9 41.4 %all-gather = f32[64,1,1024]{2,1,0:T(1,128)S(1)} all-gather(f32[1,1,1024]{2,1,0:T(1,128)S(1)} %reshape.121), channel_id=1, replica_groups=mesh['vocab'=64,'width'=8] {'vocab'}, dimensions={0}, use_global_device_ids=true | all-gather | bytes 266240 | tf_op jit(solution)/shard_map/all_gather | solution.py:33
  216.4 37.1 %all-gather.1 = f32[64,1,1024]{2,1,0:T(1,128)S(1)} all-gather(f32[1,1,1024]{2,1,0:T(1,128)S(1)} %reshape.123), channel_id=1, replica_groups=mesh['vocab'=64,'width'=8] {'vocab'}, dimensions={0}, use_global_device_ids=true | all-gather | bytes 266240 | tf_op jit(solution)/shard_map/all_gather | solution.py:33
  253.6 36.9 %all-gather.2 = f32[64,1,1024]{2,1,0:T(1,128)S(1)} all-gather(f32[1,1,1024]{2,1,0:T(1,128)S(1)} %reshape.125), channel_id=1, replica_groups=mesh['vocab'=64,'width'=8] {'vocab'}, dimensions={0}, use_global_device_ids=true | all-gather | bytes 266240 | tf_op jit(solution)/shard_map/all_gather | solution.py:33
  290.6 37.3 %all-gather.3 = f32[64,1,1024]{2,1,0:T(1,128)S(1)} all-gather(f32[1,1,1024]{2,1,0:T(1,128)S(1)} %reshape.127), channel_id=1, replica_groups=mesh['vocab'=64,'width'=8] {'vocab'}, dimensions={0}, use_global_device_ids=true | all-gather | bytes 266240 | tf_op jit(solution)/shard_map/all_gather | solution.py:33
  328.2 7.6 %while.33 = (s32[]{:T(128)}, f32[1024]{0:T(1024)S(1)}, f32[1024]{0:T(1024)S(1)}, f32[1024]{0:T(1024)S(1)}, f32[1024]{0:T(1024)S(1)}, /*index=5*/f32[63,1024]{1,0...) while((s32[]{:T(128)}, f32[1024]{0:T(1024)S(1)}, ...), condition=%wide.region_9.10_spmd, body=%wide.region_8.9_spmd.sunk | while | flops 16386 | bytes 110701 | solution.py:36
  335.7 0.6 subtract_multiply_fusion
  336.3 0.1 select_reduce_fusion.1
  336.4 96.9 %psum.15 = f32[64]{0:T(128)S(1)} all-reduce(f32[64]{0:T(128)S(1)} %select_reduce_fusion.1), channel_id=1, replica_groups=mesh['vocab'=64,'width'=8] {'vocab','width'}, use_global_device_ids=true, to_apply=%region_12.13 | all-reduce | flops 64 | bytes 512 | tf_op jit(solution)/shard_map/psum | solution.py:115
  433.3 0.5 convert_divide_fusion
  (430 shorter events, 4.7 us)
Async XLA Ops:
  7.2 129.4 %copy-start = (bf16[1600,256]{1,0:T(8,128)(2,1)S(1)}, bf16[1600,256]{1,0:T(8,128)(2,1)}, u32[]{:S(2)}) copy-start(bf16[1600,256]{1,0:T(8,128)(2,1)} %param.12) | copy-start | bytes 2457604
  7.2 151.6 %all-gather.6.cloned.1.call-start = ((), (), s32[]{:S(2)}) async-start(), calls=%async_computation.1 | async-start | bytes 4259840 | tf_op jit(solution)/shard_map/all_gather | solution.py:73
  40.3 17.2 %collective-permute-start = (bf16[1600,256]{1,0:T(8,128)(2,1)}, bf16[1600,256]{1,0:T(8,128)(2,1)S(1)}, u32[]{:S(2)}, u32[]{:S(2)}) collective-permute-start(bf16[1600,256]{1,0:T(8,128)(2,1)} %param.12), channel_id=1, source_target_pairs={{0,1},{1,2},{2,3},{3,4},{4,5},{5,6},{6,7},{7,0},{8,9},{9,10},{10,1... | collective-permute-start | bytes 2457608 | tf_op jit(solution)/shard_map/ppermute | solution.py:23
  57.6 16.7 %collective-permute-start.1 = (bf16[1600,256]{1,0:T(8,128)(2,1)S(1)}, bf16[1600,256]{1,0:T(8,128)(2,1)S(1)}, u32[]{:S(2)}, u32[]{:S(2)}) collective-permute-start(bf16[1600,256]{1,0:T(8,128)(2,1)S(1)} %collective-permute-done), channel_id=1, source_target_pairs={{0,1},{1,2},{2,3},{3,4},{4,5},{5,6},{6,7},{7,0},{8,9},{9,10},{10,1... | collective-permute-start | bytes 2457608 | tf_op jit(solution)/shard_map/ppermute | solution.py:23
  59.5 16.7 %collective-permute-start.4 = (bf16[1600,256]{1,0:T(8,128)(2,1)}, bf16[1600,256]{1,0:T(8,128)(2,1)S(1)}, u32[]{:S(2)}, u32[]{:S(2)}) collective-permute-start(bf16[1600,256]{1,0:T(8,128)(2,1)} %param.12), channel_id=1, source_target_pairs={{1,0},{2,1},{3,2},{4,3},{5,4},{6,5},{7,6},{0,7},{9,8},{10,9},{11,1... | collective-permute-start | bytes 2457608 | tf_op jit(solution)/shard_map/ppermute | solution.py:25
  74.3 16.8 %collective-permute-start.2 = (bf16[1600,256]{1,0:T(8,128)(2,1)S(1)}, bf16[1600,256]{1,0:T(8,128)(2,1)}, u32[]{:S(2)}, u32[]{:S(2)}) collective-permute-start(bf16[1600,256]{1,0:T(8,128)(2,1)S(1)} %collective-permute-done.1), channel_id=1, source_target_pairs={{0,1},{1,2},{2,3},{3,4},{4,5},{5,6},{6,7},{7,0},{8,9},{9,10},{10,1... | collective-permute-start | bytes 2457608 | tf_op jit(solution)/shard_map/ppermute | solution.py:23
  76.2 49.2 %collective-permute-start.5 = (bf16[1600,256]{1,0:T(8,128)(2,1)S(1)}, bf16[1600,256]{1,0:T(8,128)(2,1)}, u32[]{:S(2)}, u32[]{:S(2)}) collective-permute-start(bf16[1600,256]{1,0:T(8,128)(2,1)S(1)} %collective-permute-done.4), channel_id=1, source_target_pairs={{1,0},{2,1},{3,2},{4,3},{5,4},{6,5},{7,6},{0,7},{9,8},{10,9},{11,1... | collective-permute-start | bytes 2457608 | tf_op jit(solution)/shard_map/ppermute | solution.py:25
  91.1 39.4 %collective-permute-start.3 = (bf16[1600,256]{1,0:T(8,128)(2,1)}, bf16[1600,256]{1,0:T(8,128)(2,1)}, u32[]{:S(2)}, u32[]{:S(2)}) collective-permute-start(bf16[1600,256]{1,0:T(8,128)(2,1)} %collective-permute-done.2), channel_id=1, source_target_pairs={{0,1},{1,2},{2,3},{3,4},{4,5},{5,6},{6,7},{7,0},{8,9},{9,10},{10,1... | collective-permute-start | bytes 2457608 | tf_op jit(solution)/shard_map/ppermute | solution.py:23
  125.4 19.4 %collective-permute-start.6 = (bf16[1600,256]{1,0:T(8,128)(2,1)}, bf16[1600,256]{1,0:T(8,128)(2,1)S(1)}, u32[]{:S(2)}, u32[]{:S(2)}) collective-permute-start(bf16[1600,256]{1,0:T(8,128)(2,1)} %collective-permute-done.5), channel_id=1, source_target_pairs={{1,0},{2,1},{3,2},{4,3},{5,4},{6,5},{7,6},{0,7},{9,8},{10,9},{11,1... | collective-permute-start | bytes 2457608 | tf_op jit(solution)/shard_map/ppermute | solution.py:25
  158.8 177.0 %copy-start.3 = (s32[16]{0:T(128)S(1)}, s32[16]{0:T(128)}, u32[]{:S(2)}) copy-start(s32[16]{0:T(128)} %param.14) | copy-start | bytes 196
  158.8 274.6 %copy-start.2 = (s32[64]{0:T(128)S(1)}, s32[64]{0:T(128)}, u32[]{:S(2)}) copy-start(s32[64]{0:T(128)} %param.15) | copy-start | bytes 772
  336.3 97.5 %copy-start.1 = (f32[16]{0:T(128)}, f32[16]{0:T(128)S(1)}, u32[]{:S(2)}) copy-start(f32[16]{0:T(128)S(1)} %get-tuple-element.158) | copy-start | bytes 196
Sparse Core Ops, SparseCore 0:
  40.5 85.8 all-gather.5
